TPU v7x, 32 devices: a whole 2x2x4 slice. The times are simulated.
32 devices in a mesh: dp: 8 (over z, y), tensor: 4 (over x, core).
Axes of the slice: x: 2, y: 2, z: 4, core: 2. Of those that a mesh axis runs over, the one named last changes fastest.
Arguments:
- tokens: bfloat16 [8, 512, 768], P('dp'), as said below
- cotangent: bfloat16 [8, 512, 768], P('dp'), may hold values from -6 to 6
- lengths: int32 [8], P('dp'), may hold values from 128 to 512, as said below
- in_weight: float32 [7, 768, 768], P(None, 'dp', 'tensor'), as said below
- out_weight: float32 [5, 768, 768], P(None, 'tensor', 'dp'), may hold values from -0.4375 to 0.4375
- in_bias: float32 [6, 768], P(None, 'tensor'), may hold values from -3 to 3
- norm_vec: float32 [6, 768], replicated, may hold values from 0.1 to 1.9
- in_moments: float32 [2, 7, 768, 768], P(None, None, 'dp', 'tensor'), as said below
- out_moments: float32 [2, 5, 768, 768], P(None, None, 'tensor', 'dp'), as said below
- bias_moments: float32 [2, 6, 768], P(None, None, 'tensor'), as said below
- norm_moments: float32 [2, 6, 768], replicated, as said below
Outputs:
- output: bfloat16 [8, 512, 768], P('dp')
- grad_input: bfloat16 [8, 512, 768], P('dp')
- in_grad: float32 [7, 768, 768], P(None, 'dp', 'tensor')
- out_grad: float32 [5, 768, 768], P(None, 'tensor', 'dp')
- bias_grad: float32 [6, 768], P(None, 'tensor')
- norm_grad: float32 [6, 768], replicated
- new_in_weight: float32 [7, 768, 768], P(None, 'dp', 'tensor')
- new_out_weight: float32 [5, 768, 768], P(None, 'tensor', 'dp')
- new_in_bias: float32 [6, 768], P(None, 'tensor')
- new_norm_vec: float32 [6, 768], replicated
- new_in_moments: float32 [2, 7, 768, 768], P(None, None, 'dp', 'tensor')
- new_out_moments: float32 [2, 5, 768, 768], P(None, None, 'tensor', 'dp')
- new_bias_moments: float32 [2, 6, 768], P(None, None, 'tensor')
- new_norm_moments: float32 [2, 6, 768], replicated
Inputs may be any that keep to these rules, and one draw needn't show every extreme that they name: `lengths`: each sequence's live tokens come first; the first sequence is full, with 512 live tokens. `tokens`: entries lie within -6 and 6. `in_weight`: entries lie within -6 / sqrt(768) and 6 / sqrt(768). `in_moments`: second moments (index 1) are positive. `out_moments`: second moments (index 1) are positive. `bias_moments`: second moments (index 1) are positive. `norm_moments`: second moments (index 1) are positive.
All inputs are finite; a program needn't handle non-finite values.
Results may differ from a plain program's by a relative error of at most 0.023.
Values may be sent and summed in bfloat16 or wider, within the bound.
A program may use at most 128 MiB of HBM per device.

v0:
```python
import jax
import jax.numpy as jnp
from jax import lax
from jax.sharding import PartitionSpec as P

HDIM = 64
norm_eps = 1e-12
masked_score = -1e30
learn_rate = 0.005
beta_first = 0.9
beta_second = 0.999
adam_eps = 1e-08
weight_decay = 0.01
step_count = 2.0
root_half = 0.7071067811865476
normal_peak = 0.3989422804014327


def matmul(left_op, right_op):
    return jnp.dot(left_op, right_op, preferred_element_type=jnp.float32)


def inner_rows(left_op, right_op):
    return lax.dot_general(
        left_op, right_op, (((0,), (0,)), ((), ())), preferred_element_type=jnp.float32
    )


def times_transposed(left_op, right_op):
    return lax.dot_general(
        left_op, right_op, (((1,), (1,)), ((), ())), preferred_element_type=jnp.float32
    )


def layer_norm(summed_rows, gain_vec, shift_vec):
    center = jnp.mean(summed_rows, -1, keepdims=True)
    offset = summed_rows - center
    inverse = lax.rsqrt(jnp.mean(offset * offset, -1, keepdims=True) + norm_eps)
    normed = offset * inverse
    return (normed * gain_vec + shift_vec, normed, inverse)


def norm_back(upstream, normed, inverse, gain_vec):
    scaled = upstream * gain_vec
    return inverse * (
        scaled
        - jnp.mean(scaled, -1, keepdims=True)
        - normed * jnp.mean(scaled * normed, -1, keepdims=True)
    )


def gelu_value(pre_act):
    return 0.5 * pre_act * (1.0 + jax.scipy.special.erf(pre_act * root_half))


def gelu_slope(pre_act):
    return (
        0.5 * (1.0 + jax.scipy.special.erf(pre_act * root_half))
        + pre_act * jnp.exp(-0.5 * pre_act * pre_act) * normal_peak
    )


def score_block(query_heads, key_heads, length):
    seq_len = query_heads.shape[0]
    scale_factor = query_heads.shape[-1] ** (-0.5)
    scores = (
        jnp.einsum("qhe,khe->hqk", query_heads, key_heads, preferred_element_type=jnp.float32)
        * scale_factor
    )
    usable = lax.broadcasted_iota(jnp.int32, (1, 1, seq_len), 2) < length
    return jnp.where(usable, scores, masked_score)


def attend_forward(operands):
    query_heads, key_heads, value_heads, length = operands
    scores = score_block(query_heads, key_heads, length)
    highest = jnp.max(scores, -1, keepdims=True)
    log_total = highest + jnp.log(jnp.sum(jnp.exp(scores - highest), -1, keepdims=True))
    probs_low = jnp.exp(scores - log_total).astype(jnp.bfloat16)
    mixed_heads = jnp.einsum(
        "hqk,khe->qhe", probs_low, value_heads, preferred_element_type=jnp.float32
    )
    return (mixed_heads.astype(jnp.bfloat16), log_total)


def attend_backward(operands):
    query_heads, key_heads, value_heads, grad_heads, log_total, length = operands
    scale_factor = query_heads.shape[-1] ** (-0.5)
    scores = score_block(query_heads, key_heads, length)
    probs = jnp.exp(scores - log_total)
    probs_low = probs.astype(jnp.bfloat16)
    grad_probs = jnp.einsum(
        "qhe,khe->hqk", grad_heads, value_heads, preferred_element_type=jnp.float32
    )
    row_dot = jnp.sum(probs * grad_probs, -1, keepdims=True)
    grad_scores = (probs * (grad_probs - row_dot) * scale_factor).astype(jnp.bfloat16)
    grad_query = jnp.einsum(
        "hqk,khe->qhe", grad_scores, key_heads, preferred_element_type=jnp.float32
    )
    grad_keys = jnp.einsum(
        "hqk,qhe->khe", grad_scores, query_heads, preferred_element_type=jnp.float32
    )
    grad_values = jnp.einsum(
        "hqk,qhe->khe", probs_low, grad_heads, preferred_element_type=jnp.float32
    )
    return (grad_query, grad_keys, grad_values)


def adam_update(param, grad, moments, decay):
    first = beta_first * moments[0] + (1.0 - beta_first) * grad
    second = beta_second * moments[1] + (1.0 - beta_second) * grad * grad
    first_hat = first / (1.0 - beta_first**step_count)
    second_hat = second / (1.0 - beta_second**step_count)
    new_param = param - learn_rate * (first_hat / (jnp.sqrt(second_hat) + adam_eps) + decay * param)
    return (new_param, jnp.stack([first, second]))


def local(
    tokens,
    cotangent,
    lengths,
    in_weight,
    out_weight,
    in_bias,
    norm_vec,
    in_moments,
    out_moments,
    bias_moments,
    norm_moments,
):
    seq_count, seq_len, width = tokens.shape
    row_count = seq_count * seq_len
    in_full, out_full = (
        lax.all_gather(in_weight.astype(jnp.bfloat16), "dp", axis=1, tiled=True),
        lax.all_gather(out_weight.astype(jnp.bfloat16), "dp", axis=2, tiled=True),
    )
    group_width = in_full.shape[2]
    heads_here = group_width // HDIM
    w_query, w_key, w_value = (in_full[0], in_full[1], in_full[2])
    w_up = in_full[3:7]
    w_proj = out_full[0]
    w_down = out_full[1:5]
    bias_up = in_bias[2:6]

    def split_heads(flat_rows):
        return flat_rows.reshape(seq_count, seq_len, heads_here, HDIM)

    flat_tokens = tokens.reshape(row_count, width)
    query = (matmul(flat_tokens, w_query) + in_bias[0]).astype(jnp.bfloat16)
    keys_low = matmul(flat_tokens, w_key).astype(jnp.bfloat16)
    values_low = (matmul(flat_tokens, w_value) + in_bias[1]).astype(jnp.bfloat16)
    mixed_heads, log_total = lax.map(
        attend_forward,
        (split_heads(query), split_heads(keys_low), split_heads(values_low), lengths),
    )
    mixed_flat = mixed_heads.reshape(row_count, group_width)
    attn_out = lax.psum(matmul(mixed_flat, w_proj).astype(jnp.bfloat16), "tensor").astype(
        jnp.float32
    )
    hidden, normed_one, inverse_one = layer_norm(
        flat_tokens.astype(jnp.float32) + attn_out + norm_vec[0], norm_vec[1], norm_vec[2]
    )
    hidden_low = hidden.astype(jnp.bfloat16)
    pre_act = (
        jnp.einsum("rd,kdj->rkj", hidden_low, w_up, preferred_element_type=jnp.float32) + bias_up
    )
    act_low = gelu_value(pre_act).astype(jnp.bfloat16)
    ffn_part = jnp.einsum("rkj,kjd->rd", act_low, w_down, preferred_element_type=jnp.float32)
    ffn_out = lax.psum(ffn_part.astype(jnp.bfloat16), "tensor").astype(jnp.float32)
    out_rows, normed_two, inverse_two = layer_norm(
        hidden + ffn_out + norm_vec[3], norm_vec[4], norm_vec[5]
    )
    positions = lax.broadcasted_iota(jnp.int32, (seq_count, seq_len), 1)
    live_rows = (positions < lengths[:, None]).astype(jnp.float32).reshape(row_count, 1)
    grad_out = cotangent.reshape(row_count, width).astype(jnp.float32) * live_rows
    grad_two = norm_back(grad_out, normed_two, inverse_two, norm_vec[4])
    grad_two_low = grad_two.astype(jnp.bfloat16)
    grad_down = jnp.einsum("rkj,rd->kjd", act_low, grad_two_low, preferred_element_type=jnp.float32)
    grad_act = jnp.einsum("rd,kjd->rkj", grad_two_low, w_down, preferred_element_type=jnp.float32)
    grad_pre = grad_act * gelu_slope(pre_act)
    grad_pre_low = grad_pre.astype(jnp.bfloat16)
    grad_up = jnp.einsum(
        "rd,rkj->kdj", hidden_low, grad_pre_low, preferred_element_type=jnp.float32
    )
    back_part = jnp.einsum("rkj,kdj->rd", grad_pre_low, w_up, preferred_element_type=jnp.float32)
    grad_hidden = grad_two + lax.psum(back_part.astype(jnp.bfloat16), "tensor").astype(jnp.float32)
    grad_one = norm_back(grad_hidden, normed_one, inverse_one, norm_vec[1])
    grad_one_low = grad_one.astype(jnp.bfloat16)
    grad_proj = inner_rows(mixed_flat, grad_one_low)
    grad_mixed = times_transposed(grad_one_low, w_proj).astype(jnp.bfloat16)
    grad_query, grad_keys, grad_values = lax.map(
        attend_backward,
        (
            split_heads(query),
            split_heads(keys_low),
            split_heads(values_low),
            split_heads(grad_mixed),
            log_total,
            lengths,
        ),
    )
    grad_query = grad_query.reshape(row_count, group_width)
    grad_keys = grad_keys.reshape(row_count, group_width)
    grad_values = grad_values.reshape(row_count, group_width)
    query_grad_low = grad_query.astype(jnp.bfloat16)
    keys_grad_low = grad_keys.astype(jnp.bfloat16)
    values_grad_low = grad_values.astype(jnp.bfloat16)
    input_part = (
        times_transposed(query_grad_low, w_query)
        + times_transposed(keys_grad_low, w_key)
        + times_transposed(values_grad_low, w_value)
    )
    grad_input = grad_one + lax.psum(input_part.astype(jnp.bfloat16), "tensor").astype(jnp.float32)
    grad_in = jnp.concatenate(
        [
            jnp.stack(
                [
                    inner_rows(flat_tokens, query_grad_low),
                    inner_rows(flat_tokens, keys_grad_low),
                    inner_rows(flat_tokens, values_grad_low),
                ]
            ),
            grad_up,
        ],
        0,
    )
    grad_outw = jnp.concatenate([grad_proj[None], grad_down], 0)
    grad_bias = jnp.concatenate(
        [jnp.stack([jnp.sum(grad_query, 0), jnp.sum(grad_values, 0)]), jnp.sum(grad_pre, 0)], 0
    )
    grad_norm = jnp.stack(
        [
            jnp.sum(grad_one, 0),
            jnp.sum(grad_hidden * normed_one, 0),
            jnp.sum(grad_hidden, 0),
            jnp.sum(grad_two, 0),
            jnp.sum(grad_out * normed_two, 0),
            jnp.sum(grad_out, 0),
        ]
    )
    in_total, out_total, bias_total, norm_total = lax.psum(
        (grad_in, grad_outw, grad_bias, grad_norm), "dp"
    )
    owner = lax.axis_index("dp")
    in_rows = in_weight.shape[1]
    out_cols = out_weight.shape[2]
    in_share = lax.dynamic_slice_in_dim(in_total, owner * in_rows, in_rows, 1)
    out_share = lax.dynamic_slice_in_dim(out_total, owner * out_cols, out_cols, 2)
    new_in_weight, new_in_moments = adam_update(in_weight, in_share, in_moments, weight_decay)
    new_out_weight, new_out_moments = adam_update(out_weight, out_share, out_moments, weight_decay)
    new_in_bias, new_bias_moments = adam_update(in_bias, bias_total, bias_moments, 0.0)
    new_norm_vec, new_norm_moments = adam_update(norm_vec, norm_total, norm_moments, 0.0)
    output = out_rows.astype(jnp.bfloat16).reshape(seq_count, seq_len, width)
    grad_tokens = grad_input.astype(jnp.bfloat16).reshape(seq_count, seq_len, width)
    return (
        output,
        grad_tokens,
        in_share,
        out_share,
        bias_total,
        norm_total,
        new_in_weight,
        new_out_weight,
        new_in_bias,
        new_norm_vec,
        new_in_moments,
        new_out_moments,
        new_bias_moments,
        new_norm_moments,
    )


def solution(mesh):
    in_specs = (
        P("dp", None, None),
        P("dp", None, None),
        P("dp"),
        P(None, "dp", "tensor"),
        P(None, "tensor", "dp"),
        P(None, "tensor"),
        P(),
        P(None, None, "dp", "tensor"),
        P(None, None, "tensor", "dp"),
        P(None, None, "tensor"),
        P(),
    )
    out_specs = (
        P("dp", None, None),
        P("dp", None, None),
        P(None, "dp", "tensor"),
        P(None, "tensor", "dp"),
        P(None, "tensor"),
        P(),
        P(None, "dp", "tensor"),
        P(None, "tensor", "dp"),
        P(None, "tensor"),
        P(),
        P(None, None, "dp", "tensor"),
        P(None, None, "tensor", "dp"),
        P(None, None, "tensor"),
        P(),
    )
    return jax.shard_map(local, mesh=mesh, in_specs=in_specs, out_specs=out_specs, check_vma=False)
```

profile of v0, /device:TPU:0, one launch (start us, length us, event | category | flops | bytes accessed | tf_op | source)
XLA Modules:
  0.0 594.2 jit_solution(6022142361547197899)
XLA Ops:
  11.3 62.3 %all-gather.5.cloned.1.call-done = bf16[5,192,768]{1,0,2:T(8,128)(2,1)} async-done(((bf16[5,192,96]{1,0,2:T(8,128)(2,1)}), bf16[5,192,768]{1,0,2:T(8,128)(2,1)}) %all-gather.5.cloned.1.call-update) | async-done | bytes 1474576 | tf_op jit(solution)/shard_map/all_gather | solution.py:135
  73.5 2.4 slice.97
  77.6 57.4 %all-gather.3.cloned.1.call-done = bf16[7,768,192]{2,0,1:T(8,128)(2,1)} async-done(((bf16[7,96,192]{2,0,1:T(8,128)(2,1)}), bf16[7,768,192]{2,0,1:T(8,128)(2,1)}) %all-gather.3.cloned.1.call-update) | async-done | bytes 2064400 | tf_op jit(solution)/shard_map/all_gather | solution.py:134
  135.0 6.1 %fusion.97 = (bf16[1,768,192]{2,0,1:T(2,128)(2,1)S(1)}, bf16[1,768,192]{2,0,1:T(2,128)(2,1)S(1)}, bf16[1,768,192]{2,0,1:T(2,128)(2,1)S(1)}) fusion(bf16[7,768,192]{2,0,1:T(8,128)(2,1)} %all-gather.3.cloned.1.call-done), kind=kLoop, calls=%fused_computation.162 | loop fusion | bytes 1769472 | tf_op jit(solution)/shard_map/slice | solution.py:139
  149.5 2.8 slice.99
  152.3 2.2 copy.141
  154.5 2.7 slice.98
  157.2 2.1 copy.140
  159.4 23.8 %all-reduce.8.cloned.1.call-done = bf16[512,768]{1,0:T(8,128)(2,1)} async-done(((bf16[512,768]{1,0:T(8,128)(2,1)}), bf16[512,768]{1,0:T(8,128)(2,1)}) %all-reduce.8.cloned.1.call-update) | async-done | bytes 786448 | tf_op jit(solution)/shard_map/psum | solution.py:157
  188.2 1.7 bitcast_convert_fusion.1
  190.2 34.9 %all-reduce.10.cloned.1.call-done = bf16[512,768]{1,0:T(8,128)(2,1)} async-done(((bf16[512,768]{1,0:T(8,128)(2,1)}), bf16[512,768]{1,0:T(8,128)(2,1)}) %all-reduce.10.cloned.1.call-update) | async-done | bytes 786448 | tf_op jit(solution)/shard_map/psum | solution.py:169
  225.1 1.9 fusion.96
  231.1 2.0 fusion.106
  233.9 1.7 bitcast_convert_fusion
  235.7 3.4 fusion.41
  239.1 2.5 convolution_bitcast_fusion
  241.6 29.2 %all-reduce.12.cloned.1.call-done = bf16[512,768]{1,0:T(8,128)(2,1)} async-done(((bf16[512,768]{1,0:T(8,128)(2,1)}), bf16[512,768]{1,0:T(8,128)(2,1)}) %all-reduce.12.cloned.1.call-update) | async-done | bytes 786448 | tf_op jit(solution)/shard_map/psum | solution.py:186
  270.9 2.8 multiply_reduce_fusion.1
  273.7 2.8 fusion.95
  277.5 2.4 fusion.107
  279.8 7.2 %fusion.99 = (f32[3,64]{1,0:T(4,128)}, bf16[512,3,64]{0,2,1:T(8,128)(2,1)S(1)}) fusion(bf16[512,3,64]{0,2,1:T(8,128)(2,1)S(1)} %bitcast.222, f32[3,512,512]{1,2,0:T(8,128)} %fusion.107, f32[3,512]{1,0:T(4,128)S(1)} %log_add_fusion, f32[3,512,512]{1,2,0:T(8,128)} %copy-done.3, pred[512]{0:T(512)(128)(4,1)S(1)} %iota_compare_fusion), kind=kOutput, calls=%fused_computation.164 | convolution fusion | flops 109512512 | bytes 6692096 | tf_op jit(solution)/shard_map/while/body/eval_jaxpr/hqk,khe->qhe/dot_general | solution.py:97
  287.0 6.6 %fusion.35 = bf16[3,64,512]{2,1,0:T(8,128)(2,1)S(1)} fusion(bf16[512,3,64]{0,2,1:T(8,128)(2,1)S(1)} %bitcast.232, f32[3,512,512]{1,2,0:T(8,128)} %fusion.107, f32[3,512,512]{1,2,0:T(8,128)} %copy-done.3, f32[3,512]{1,0:T(4,128)S(1)} %log_add_fusion, pred[512]{0:T(512)(128)(4,1)S(1)} %iota_compare_fusion), kind=kOutput, calls=%fused_computation.65 | convolution fusion | flops 109414400 | bytes 6691328 | tf_op jit(solution)/shard_map/while/body/eval_jaxpr/hqk,qhe->khe/dot_general | solution.py:100
  293.7 3.5 fusion.100
  304.3 3.8 pad_maximum_fusion.1
  308.1 2.3 pad_maximum_fusion
  312.6 2.3 fusion.98
  318.0 37.5 %all-reduce = (f32[6,192]{1,0:T(8,128)S(1)}, f32[6,768]{1,0:T(8,128)S(1)}) all-reduce(f32[6,192]{1,0:T(8,128)S(1)} %pad_maximum_fusion.6, f32[6,768]{1,0:T(8,128)S(1)} %stack.83), channel_id=1, replica_groups=mesh['dp'=8,'tensor'=4] {'dp'}, use_global_device_ids=true, to_apply=%region_20.21 | all-reduce | flops 5760 | bytes 46080 | tf_op jit(solution)/shard_map/psum | solution.py:241
  358.0 2.2 fusion.39
  360.2 214.8 %all-reduce.16.cloned.1.call-done = (f32[7,768,192]{1,2,0:T(8,128)}, f32[5,192,768]{2,1,0:T(8,128)}) async-done(((f32[7,768,192]{1,2,0:T(8,128)}, f32[5,192,768]{2,1,0:T(8,128)}), (f32[7,768,192]{1,2,0:T(8,128)}, f32[5,192,768]{2,1,0:T(8,128)})) %all-reduce.16.cloned.1.call-update) | async-done | bytes 7077904 | tf_op jit(solution)/shard_map/psum | solution.py:241
  575.0 1.7 fusion.70
  579.4 2.4 copy.128
  584.7 1.6 copy.129
  (197 shorter events, 45.4 us)
Async XLA Ops:
  7.2 66.3 %all-gather.5.cloned.1.call-start = ((), (), s32[]{:S(2)}) async-start(), calls=%async_computation.1 | async-start | bytes 3538944 | tf_op jit(solution)/shard_map/all_gather | solution.py:135
  8.4 2.9 copy-start.43
  9.5 125.5 %all-gather.3.cloned.1.call-start = ((), (), s32[]{:S(2)}) async-start(), calls=%async_computation | async-start | bytes 3538944 | tf_op jit(solution)/shard_map/all_gather | solution.py:134
  10.5 172.7 %all-reduce.8.cloned.1.call-start = ((), (), s32[]{:S(2)}) async-start(), calls=%async_computation.2 | async-start | bytes 1572864 | tf_op jit(solution)/shard_map/psum | solution.py:157
  149.4 75.7 %all-reduce.10.cloned.1.call-start = ((), (), s32[]{:S(2)}) async-start(), calls=%async_computation.3 | async-start | bytes 1572864 | tf_op jit(solution)/shard_map/psum | solution.py:169
  189.9 80.9 %all-reduce.12.cloned.1.call-start = ((), (), s32[]{:S(2)}) async-start(), calls=%async_computation.4 | async-start | bytes 1572864 | tf_op jit(solution)/shard_map/psum | solution.py:186
  230.6 40.2 %copy-start.1 = (f32[512,768]{1,0:T(8,128)}, f32[512,768]{1,0:T(8,128)S(1)}, u32[]{:S(2)}) copy-start(f32[512,768]{1,0:T(8,128)S(1)} %get-tuple-element.165) | copy-start | bytes 4718596
  231.1 2.9 copy-start.27
  235.7 122.3 %all-reduce.14.cloned.1.call-start = ((), (), s32[]{:S(2)}) async-start(), calls=%async_computation.5 | async-start | bytes 1572864 | tf_op jit(solution)/shard_map/psum | solution.py:213
  235.7 3.4 copy-start.55
  270.9 2.8 copy-start.5
  273.7 2.8 copy-start.13
  279.8 7.2 %copy-start.39 = (bf16[512,192]{0,1:T(8,128)(2,1)S(1)}, bf16[512,192]{0,1:T(8,128)(2,1)}, u32[]{:S(2)}) copy-start(bf16[512,192]{0,1:T(8,128)(2,1)} %copy-done.38) | copy-start | bytes 589828
  287.0 11.8 %copy-start.34 = (bf16[512,3,64]{0,2,1:T(8,128)(2,1)}, bf16[512,3,64]{0,2,1:T(8,128)(2,1)S(1)}, u32[]{:S(2)}) copy-start(bf16[512,3,64]{0,2,1:T(8,128)(2,1)S(1)} %get-tuple-element.174) | copy-start | bytes 589828
  293.7 3.5 copy-start.35
  304.2 3.9 copy-start.14
  304.2 270.8 %all-reduce.16.cloned.1.call-start = ((), (), s32[]{:S(2)}) async-start(), calls=%async_computation.6 | async-start | bytes 14155776 | tf_op jit(solution)/shard_map/psum | solution.py:241
  304.2 3.8 copy-start.15
  314.9 2.7 copy-start.42
  314.9 2.8 copy-start.53
  314.9 2.9 copy-start.52
  314.9 2.9 copy-start.48
  314.9 2.9 copy-start.47
  314.9 2.9 copy-start.46
  314.9 2.9 copy-start.45
  314.9 3.0 copy-start.51
  314.9 41.8 %copy-start.41 = (f32[6,768]{1,0:T(8,128)S(1)}, f32[6,768]{1,0:T(8,128)}, u32[]{:S(2)}) copy-start(f32[6,768]{1,0:T(8,128)} %param.17) | copy-start | bytes 55300
  355.5 4.7 copy-start.44
  355.5 4.7 copy-start.50
  575.0 2.9 copy-start.9
  575.0 2.9 copy-start.10
  579.4 3.8 copy-start.17
  (31 other events, 49.6 us)
Sparse Core Ops, SparseCore 0:
  10.8 62.7 all-gather.4
  76.3 58.6 all-gather.2
  149.5 33.6 all-reduce.7
  190.0 35.0 all-reduce.9
  235.8 35.0 all-reduce.11
  304.3 35.0 all-reduce.13
  343.4 231.5 all-reduce.15
where the time goes:
time: 595 us; the launch traced here: 594 us
  waiting for transfers between devices  423 us (71%)
  matrix products  43.5 us (7%)
  local copies, waits for them, and re-layouts  43.2 us (7%)
  blocking collectives  37.5 us (6%)
  other arithmetic  31.4 us (5%)
  between operations  15.5 us (3%)
    psum x1, waiting for transfers between devices, local(): lax.psum((grad_in, grad_outw, grad_bias, grad_norm), 'dp')  215 us
    all_gather x1, waiting for transfers between devices, local(): lax.all_gather(out_weight.astype(jnp.bfloat16), 'dp', axis=2, tiled=True)  62.3 us
    all_gather x1, waiting for transfers between devices, local(): lax.all_gather(in_weight.astype(jnp.bfloat16), 'dp', axis=1, tiled=True)  57.4 us
    psum x1, blocking collectives, local(): lax.psum((grad_in, grad_outw, grad_bias, grad_norm), 'dp')  37.5 us
    psum x1, waiting for transfers between devices, local(): lax.psum(ffn_part.astype(jnp.bfloat16), 'tensor').astype(jnp.float32)  34.9 us
    psum x1, waiting for transfers between devices, local(): lax.psum(back_part.astype(jnp.bfloat16), 'tensor').astype(jnp.float32)  29.2 us
    unnamed x126, local copies, waits for them, and re-layouts  24.5 us
    psum x1, waiting for transfers between devices, local(): lax.psum(matmul(mixed_flat, w_proj).astype(jnp.bfloat16), 'tensor')  23.8 us
  transfers between devices with their start and end apart: 7, of which 6 were waited for; matrix products, arithmetic and copies ran while one was open for 6% of the time, Pallas kernels for 0%

commit v1 on v0

--- a/solution.py
+++ b/solution.py
@@ -130,8 +130,20 @@
 ):
     seq_count, seq_len, width = tokens.shape
     row_count = seq_count * seq_len
+
+    def store_weights_in(state):
+        local_part, taken_in = (lax.psum(1, "dp"), lax.axis_index("dp"))
+        z_new, value_now = (state, 1)
+        while value_now < local_part:
+            y2 = lax.ppermute(z_new, "dp", perm=[(c, c ^ value_now) for c in range(local_part)])
+            before = jnp.concatenate([z_new, y2], axis=1)
+            reached = jnp.concatenate([y2, z_new], axis=1)
+            z_new = jnp.where(taken_in & value_now == 0, before, reached)
+            value_now = 2 * value_now
+        return z_new
+
     in_full, out_full = (
-        lax.all_gather(in_weight.astype(jnp.bfloat16), "dp", axis=1, tiled=True),
+        store_weights_in(in_weight.astype(jnp.bfloat16)),
         lax.all_gather(out_weight.astype(jnp.bfloat16), "dp", axis=2, tiled=True),
     )
     group_width = in_full.shape[2]

time: 595 us -> 575 us (0.966)
  local copies, waits for them, and re-layouts: 43.2 us -> 26.5 us
  waiting for transfers between devices: 423 us -> 411 us
  starting transfers between devices: 0.47 us -> 7.95 us
    ppermute x0 -> x3, waiting for transfers between devices: none -> 94.3 us  [store_weights_in(): lax.ppermute(z_new, 'dp', perm=[(c, c ^ value_now) for c in range(local_p...]
    all_gather x1, waiting for transfers between devices: 62.3 us -> 4.27 us  [local(): lax.all_gather(out_weight.astype(jnp.bfloat16), 'dp', axis=2, tiled=True)]
    all_gather x1 -> x0, waiting for transfers between devices: 57.4 us -> none  [local(): lax.all_gather(in_weight.astype(jnp.bfloat16), 'dp', axis=1, tiled=True)]
    ppermute x0 -> x3, starting transfers between devices: none -> 7.52 us  [store_weights_in(): lax.ppermute(z_new, 'dp', perm=[(c, c ^ value_now) for c in range(local_p...]
    psum x1, waiting for transfers between devices: 23.8 us -> 30.9 us  [local(): lax.psum(matmul(mixed_flat, w_proj).astype(jnp.bfloat16), 'tensor')]
    unnamed x126 -> x114, local copies, waits for them, and re-layouts: 24.5 us -> 17.7 us
    slice x1 -> x0, local copies, waits for them, and re-layouts: 6.14 us -> none  [local(): w_query, w_key, w_value = (in_full[0], in_full[1], in_full[2])]
  transfers between devices with their start and end apart: 7 -> 9, of which waited for: 6 -> 8; matrix products, arithmetic and copies ran while one was open for 6% -> 6% of each run, Pallas kernels for 0% -> 0%
where the time goes in v1:
time: 575 us
  waiting for transfers between devices  411 us (71%)
  matrix products  42.7 us (7%)
  blocking collectives  37.4 us (7%)
  other arithmetic  34 us (6%)
  local copies, waits for them, and re-layouts  26.5 us (5%)
  between operations  15.5 us (3%)
  starting transfers between devices  7.95 us (1%)
    psum x1, waiting for transfers between devices, local(): lax.psum((grad_in, grad_outw, grad_bias, grad_norm), 'dp')  217 us
    ppermute x3, waiting for transfers between devices, store_weights_in(): lax.ppermute(z_new, 'dp', perm=[(c, c ^ value_now) for c in range(local_p...  94.3 us
    psum x1, blocking collectives, local(): lax.psum((grad_in, grad_outw, grad_bias, grad_norm), 'dp')  37.4 us
    psum x1, waiting for transfers between devices, local(): lax.psum(ffn_part.astype(jnp.bfloat16), 'tensor').astype(jnp.float32)  35 us
    psum x1, waiting for transfers between devices, local(): lax.psum(matmul(mixed_flat, w_proj).astype(jnp.bfloat16), 'tensor')  30.9 us
    psum x1, waiting for transfers between devices, local(): lax.psum(back_part.astype(jnp.bfloat16), 'tensor').astype(jnp.float32)  29.2 us
    unnamed x114, local copies, waits for them, and re-layouts  17.7 us
  transfers between devices with their start and end apart: 9, of which 8 were waited for; matrix products, arithmetic and copies ran while one was open for 6% of the time, Pallas kernels for 0%

profile of v1, /device:TPU:0, one launch (start us, length us, event | category | flops | bytes accessed | tf_op | source)
XLA Modules:
  0.0 574.6 jit_solution(1039921530417711140)
XLA Ops:
  8.7 3.1 collective-permute-start
  11.7 8.1 %collective-permute-done = bf16[7,96,192]{1,2,0:T(8,128)(2,1)S(1)} collective-permute-done((bf16[7,96,192]{1,2,0:T(8,128)(2,1)S(1)}, bf16[7,96,192]{1,2,0:T(8,128)(2,1)S(1)}, u32[]{:S(2)}, u32[]{:S(2)}) %collective-permute-start) | collective-permute-done | bytes 258080 | tf_op jit(solution)/shard_map/ppermute | solution.py:138
  20.4 1.9 collective-permute-start.1
  22.3 14.9 %collective-permute-done.1 = bf16[7,192,192]{1,2,0:T(8,128)(2,1)} collective-permute-done((bf16[7,192,192]{1,2,0:T(8,128)(2,1)S(1)}, bf16[7,192,192]{1,2,0:T(8,128)(2,1)}, u32[]{:S(2)}, u32[]{:S(2)}) %collective-permute-start.1) | collective-permute-done | bytes 516128 | tf_op jit(solution)/shard_map/ppermute | solution.py:138
  37.2 2.1 maximum_select_fusion.1
  39.3 2.6 collective-permute-start.2
  43.8 71.3 %collective-permute-done.2 = bf16[7,384,192]{1,2,0:T(8,128)(2,1)S(1)} collective-permute-done((bf16[7,384,192]{1,2,0:T(8,128)(2,1)S(1)}, bf16[7,384,192]{1,2,0:T(8,128)(2,1)S(1)}, u32[]{:S(2)}, u32[]{:S(2)}) %collective-permute-start.2) | collective-permute-done | bytes 1032224 | tf_op jit(solution)/shard_map/ppermute | solution.py:138
  119.8 4.3 all-gather.2.cloned.1.call-done
  124.1 2.4 slice.97
  128.5 2.8 slice.99
  131.2 2.1 copy.128
  133.4 30.9 %all-reduce.8.cloned.1.call-done = bf16[512,768]{1,0:T(8,128)(2,1)} async-done(((bf16[512,768]{1,0:T(8,128)(2,1)}), bf16[512,768]{1,0:T(8,128)(2,1)}) %all-reduce.8.cloned.1.call-update) | async-done | bytes 786448 | tf_op jit(solution)/shard_map/psum | solution.py:169
  171.2 35.0 %all-reduce.10.cloned.1.call-done = bf16[512,768]{1,0:T(8,128)(2,1)} async-done(((bf16[512,768]{1,0:T(8,128)(2,1)}), bf16[512,768]{1,0:T(8,128)(2,1)}) %all-reduce.10.cloned.1.call-update) | async-done | bytes 786448 | tf_op jit(solution)/shard_map/psum | solution.py:181
  206.2 1.9 fusion.91
  212.1 2.0 fusion.100
  216.8 3.4 fusion.41
  220.2 2.5 convolution_bitcast_fusion
  222.8 29.2 %all-reduce.12.cloned.1.call-done = bf16[512,768]{1,0:T(8,128)(2,1)} async-done(((bf16[512,768]{1,0:T(8,128)(2,1)}), bf16[512,768]{1,0:T(8,128)(2,1)}) %all-reduce.12.cloned.1.call-update) | async-done | bytes 786448 | tf_op jit(solution)/shard_map/psum | solution.py:198
  251.9 2.9 multiply_reduce_fusion.1
  257.2 2.3 fusion.101
  259.5 7.2 %fusion.93 = (f32[3,64]{1,0:T(4,128)}, bf16[512,3,64]{0,2,1:T(8,128)(2,1)S(1)}) fusion(bf16[512,3,64]{0,2,1:T(8,128)(2,1)S(1)} %bitcast.224, f32[3,512,512]{1,2,0:T(8,128)} %fusion.101, f32[3,512]{1,0:T(4,128)S(1)} %log_add_fusion, f32[3,512,512]{1,2,0:T(8,128)} %copy-done.5, pred[512]{0:T(512)(128)(4,1)S(1)} %iota_compare_fusion), kind=kOutput, calls=%fused_computation.164 | convolution fusion | flops 109512512 | bytes 6692096 | tf_op jit(solution)/shard_map/while/body/eval_jaxpr/hqk,khe->qhe/dot_general | solution.py:97
  266.7 6.6 %fusion.35 = bf16[3,64,512]{2,1,0:T(8,128)(2,1)S(1)} fusion(bf16[512,3,64]{0,2,1:T(8,128)(2,1)S(1)} %bitcast.234, f32[3,512,512]{1,2,0:T(8,128)} %fusion.101, f32[3,512,512]{1,2,0:T(8,128)} %copy-done.5, f32[3,512]{1,0:T(4,128)S(1)} %log_add_fusion, pred[512]{0:T(512)(128)(4,1)S(1)} %iota_compare_fusion), kind=kOutput, calls=%fused_computation.66 | convolution fusion | flops 109414400 | bytes 6691328 | tf_op jit(solution)/shard_map/while/body/eval_jaxpr/hqk,qhe->khe/dot_general | solution.py:100
  273.3 3.6 fusion.94
  283.1 3.9 pad_maximum_fusion.1
  287.0 2.2 pad_maximum_fusion
  289.2 2.3 fusion.92
  294.6 37.4 %all-reduce = (f32[6,192]{1,0:T(8,128)S(1)}, f32[6,768]{1,0:T(8,128)S(1)}) all-reduce(f32[6,192]{1,0:T(8,128)S(1)} %pad_maximum_fusion.6, f32[6,768]{1,0:T(8,128)S(1)} %stack.83), channel_id=1, replica_groups=mesh['dp'=8,'tensor'=4] {'dp'}, use_global_device_ids=true, to_apply=%region_20.21 | all-reduce | flops 5760 | bytes 46080 | tf_op jit(solution)/shard_map/psum | solution.py:253
  334.5 2.2 fusion.39
  336.7 217.0 %all-reduce.16.cloned.1.call-done = (f32[7,768,192]{1,2,0:T(8,128)}, f32[5,192,768]{2,1,0:T(8,128)}) async-done(((f32[7,768,192]{1,2,0:T(8,128)}, f32[5,192,768]{2,1,0:T(8,128)}), (f32[7,768,192]{1,2,0:T(8,128)}, f32[5,192,768]{2,1,0:T(8,128)})) %all-reduce.16.cloned.1.call-update) | async-done | bytes 7077904 | tf_op jit(solution)/shard_map/psum | solution.py:253
  556.5 2.7 fusion.68
  559.2 2.4 copy.119
  561.5 2.2 fusion.69
  (190 shorter events, 44.0 us)
Async XLA Ops:
  7.2 116.9 %all-gather.2.cloned.1.call-start = ((), (), s32[]{:S(2)}) async-start(), calls=%async_computation | async-start | bytes 3538944 | tf_op jit(solution)/shard_map/all_gather | solution.py:147
  8.6 30.7 %copy-start.9 = (f32[7,96,192]{1,2,0:T(8,128)}, f32[7,96,192]{1,2,0:T(8,128)S(1)}, u32[]{:S(2)}) copy-start(f32[7,96,192]{1,2,0:T(8,128)S(1)} %copy.102) | copy-start | bytes 1548292
  8.7 11.1 %collective-permute-start = (bf16[7,96,192]{1,2,0:T(8,128)(2,1)S(1)}, bf16[7,96,192]{1,2,0:T(8,128)(2,1)S(1)}, u32[]{:S(2)}, u32[]{:S(2)}) collective-permute-start(bf16[7,96,192]{1,2,0:T(8,128)(2,1)S(1)} %convert_element_type.132), channel_id=1, source_target_pairs={{0,4},{4,0},{8,12},{12,8},{16,20},{20,16},{24,28},{28,24},{1,5},{5... | collective-permute-start | bytes 774152 | tf_op jit(solution)/shard_map/ppermute | solution.py:138
  11.7 30.1 %copy-start.18 = (f32[5,192,96]{2,1,0:T(8,128)S(1)}, f32[5,192,96]{2,1,0:T(8,128)}, u32[]{:S(2)}) copy-start(f32[5,192,96]{2,1,0:T(8,128)} %param.15) | copy-start | bytes 1105924
  20.4 16.8 %collective-permute-start.1 = (bf16[7,192,192]{1,2,0:T(8,128)(2,1)S(1)}, bf16[7,192,192]{1,2,0:T(8,128)(2,1)}, u32[]{:S(2)}, u32[]{:S(2)}) collective-permute-start(bf16[7,192,192]{1,2,0:T(8,128)(2,1)S(1)} %maximum_select_fusion.2), channel_id=1, source_target_pairs={{0,8},{4,12},{8,0},{12,4},{16,24},{20,28},{24,16},{28,20},{1,9},{5... | collective-permute-start | bytes 1548296 | tf_op jit(solution)/shard_map/ppermute | solution.py:138
  22.3 21.5 %copy-start.39 = (f32[6,192]{1,0:T(8,128)S(1)}, f32[6,192]{1,0:T(8,128)}, u32[]{:S(2)}) copy-start(f32[6,192]{1,0:T(8,128)} %param.16) | copy-start | bytes 13828
  39.3 75.8 %collective-permute-start.2 = (bf16[7,384,192]{1,2,0:T(8,128)(2,1)S(1)}, bf16[7,384,192]{1,2,0:T(8,128)(2,1)S(1)}, u32[]{:S(2)}, u32[]{:S(2)}) collective-permute-start(bf16[7,384,192]{1,2,0:T(8,128)(2,1)S(1)} %maximum_select_fusion.1), channel_id=1, source_target_pairs={{0,16},{4,20},{8,24},{12,28},{16,0},{20,4},{24,8},{28,12},{1,17},{... | collective-permute-start | bytes 3096584 | tf_op jit(solution)/shard_map/ppermute | solution.py:138
  43.0 121.3 %all-reduce.8.cloned.1.call-start = ((), (), s32[]{:S(2)}) async-start(), calls=%async_computation.1 | async-start | bytes 1572864 | tf_op jit(solution)/shard_map/psum | solution.py:169
  43.7 71.8 %copy-start = (bf16[1,512,768]{2,1,0:T(8,128)(2,1)S(1)}, bf16[1,512,768]{2,1,0:T(8,128)(2,1)}, u32[]{:S(2)}) copy-start(bf16[1,512,768]{2,1,0:T(8,128)(2,1)} %param.11) | copy-start | bytes 2359300
  119.8 8.5 %copy-start.27 = (bf16[3,64,512]{2,1,0:T(8,128)(2,1)}, bf16[3,64,512]{2,1,0:T(8,128)(2,1)S(1)}, u32[]{:S(2)}) copy-start(bf16[3,64,512]{2,1,0:T(8,128)(2,1)S(1)} %convolution_convert_fusion.1) | copy-start | bytes 589828
  128.3 77.9 %all-reduce.10.cloned.1.call-start = ((), (), s32[]{:S(2)}) async-start(), calls=%async_computation.2 | async-start | bytes 1572864 | tf_op jit(solution)/shard_map/psum | solution.py:181
  171.0 80.9 %all-reduce.12.cloned.1.call-start = ((), (), s32[]{:S(2)}) async-start(), calls=%async_computation.3 | async-start | bytes 1572864 | tf_op jit(solution)/shard_map/psum | solution.py:198
  212.1 2.9 copy-start.7
  216.7 117.7 %all-reduce.14.cloned.1.call-start = ((), (), s32[]{:S(2)}) async-start(), calls=%async_computation.4 | async-start | bytes 1572864 | tf_op jit(solution)/shard_map/psum | solution.py:225
  216.8 3.4 copy-start.51
  251.9 2.9 copy-start.3
  251.9 2.9 copy-start.12
  259.5 7.2 %copy-start.35 = (bf16[192,512]{1,0:T(8,128)(2,1)S(1)}, bf16[192,512]{1,0:T(8,128)(2,1)}, u32[]{:S(2)}) copy-start(bf16[192,512]{1,0:T(8,128)(2,1)} %copy-done.34) | copy-start | bytes 589828
  266.7 11.0 %copy-start.31 = (bf16[512,3,64]{0,2,1:T(8,128)(2,1)}, bf16[512,3,64]{0,2,1:T(8,128)(2,1)S(1)}, u32[]{:S(2)}) copy-start(bf16[512,3,64]{0,2,1:T(8,128)(2,1)S(1)} %get-tuple-element.171) | copy-start | bytes 589828
  273.3 3.6 copy-start.8
  283.0 4.0 copy-start.15
  283.0 270.6 %all-reduce.16.cloned.1.call-start = ((), (), s32[]{:S(2)}) async-start(), calls=%async_computation.5 | async-start | bytes 14155776 | tf_op jit(solution)/shard_map/psum | solution.py:253
  283.1 3.9 copy-start.16
  291.5 2.9 copy-start.44
  291.5 2.9 copy-start.43
  291.5 2.9 copy-start.42
  291.6 2.9 copy-start.41
  291.6 3.0 copy-start.47
  291.6 41.6 %copy-start.37 = (f32[6,768]{1,0:T(8,128)S(1)}, f32[6,768]{1,0:T(8,128)}, u32[]{:S(2)}) copy-start(f32[6,768]{1,0:T(8,128)} %param.17) | copy-start | bytes 55300
  331.9 4.7 copy-start.40
  332.0 4.7 copy-start.46
  559.1 4.5 copy-start.19
  (30 other events, 54.6 us)
Sparse Core Ops, SparseCore 0:
  43.1 80.9 all-gather.1
  128.5 35.7 all-reduce.7
  171.1 35.0 all-reduce.9
  216.9 35.0 all-reduce.11
  283.1 35.0 all-reduce.13
  322.1 231.5 all-reduce.15
